TPU v7x, 32 devices: a whole 2x2x4 slice. The times are simulated.
32 devices in a mesh: node: 8 (over z, y), local: 4 (over x, core).
Axes of the slice: x: 2, y: 2, z: 4, core: 2. Of those that a mesh axis runs over, the one named last changes fastest.
Arguments:
- inputs: bfloat16 [64, 3584], P('node', 'local'), may hold values from -6 to 6
- out_grad: bfloat16 [64, 3584], P('node', 'local'), may hold values from -6 to 6
- expert_ids: int32 [64, 2], replicated, may hold values from 0 to 7, all different within a row; in each aligned block of 64 rows (0 to 63, 64 to 127, ...) at most 32 rows name the same one
- route_probs: float32 [64, 2], replicated, may hold values from 0.1 to 1
- gate_weight: bfloat16 [8, 3584, 1024], P('node', None, 'local'), may hold values from -0.09375 to 0.09375
- up_weight: bfloat16 [8, 3584, 1024], P('node', None, 'local'), may hold values from -0.09375 to 0.09375
- down_weight: bfloat16 [8, 1024, 3584], P('node', 'local'), may hold values from -0.1875 to 0.1875
Outputs:
- d_inputs: bfloat16 [64, 3584], P('node', 'local')
Inputs may be any that keep to these rules, and one draw needn't show every extreme that they name: `expert_ids`: each row names 2 different experts. No expert is named by more than 32 pairs in all, a bound that some block reaches.
All inputs are finite; a program needn't handle non-finite values.
Results may differ from a plain program's by a relative error of at most 0.0064.
Values may be sent and summed in bfloat16 or wider, within the bound.
No kernel may reach another device: no remote copies, remote signals or barrier semaphores. Data moves between devices by JAX's collectives and lax.ppermute only.
A program may use at most 64 MiB of HBM per device.

v0:
```python
import jax
import jax.numpy as jnp
from jax import lax
from jax.sharding import PartitionSpec as P


def slot_tables(expert_ids, route_probs, expert, cape):
    flat = expert_ids.reshape(-1)
    hit = (flat == expert).astype(jnp.int32)
    rank = jnp.cumsum(hit) - 1
    slots = jnp.arange(cape, dtype=jnp.int32)
    onehot = jnp.where((rank[None, :] == slots[:, None]) & (hit[None, :] == 1), 1.0, 0.0).astype(
        jnp.float32
    )
    onehot = onehot.reshape(cape, expert_ids.shape[0], expert_ids.shape[1])
    select = jnp.sum(onehot, axis=2)
    scale = jnp.sum(onehot * route_probs[None, :, :], axis=(1, 2))
    return (select, scale)


def expert_terms(x_rows, g_rows, gate_w, up_w, down_w):
    gate = jnp.dot(x_rows, gate_w, preferred_element_type=jnp.float32)
    up = jnp.dot(x_rows, up_w, preferred_element_type=jnp.float32)
    sig = jax.nn.sigmoid(gate)
    act = gate * sig
    d_hidden = lax.dot_general(
        g_rows, down_w, (((1,), (1,)), ((), ())), preferred_element_type=jnp.float32
    )
    d_up = (d_hidden * act).astype(jnp.bfloat16)
    d_gate = (d_hidden * up * sig * (1.0 + gate * (1.0 - sig))).astype(jnp.bfloat16)
    first = lax.dot_general(
        d_gate, gate_w, (((1,), (1,)), ((), ())), preferred_element_type=jnp.float32
    )
    second = lax.dot_general(
        d_up, up_w, (((1,), (1,)), ((), ())), preferred_element_type=jnp.float32
    )
    return first + second


def shards(inputs, out_grad, expert_ids, route_probs, gate_weight, up_weight, down_weight):
    expert = lax.axis_index("node")
    tok_rows = inputs.shape[0]
    width = inputs.shape[1]
    cape = 2 * tok_rows * expert_ids.shape[1]
    select, scale = slot_tables(expert_ids, route_probs, expert, cape)
    sel_half = select.astype(jnp.bfloat16)
    every_x, every_g = (
        lax.all_gather(inputs, "node", axis=0, tiled=True),
        lax.all_gather(out_grad, "node", axis=0, tiled=True),
    )
    x_sum = jnp.dot(sel_half, every_x, preferred_element_type=jnp.float32)
    g_sum = jnp.dot(sel_half, every_g, preferred_element_type=jnp.float32)
    x_part = x_sum.astype(jnp.bfloat16)
    g_part = (scale[:, None] * g_sum).astype(jnp.bfloat16)
    x_rows, g_rows = (
        lax.all_gather(x_part, "local", axis=1, tiled=True),
        lax.all_gather(g_part, "local", axis=1, tiled=True),
    )
    partial_value = expert_terms(x_rows, g_rows, gate_weight[0], up_weight[0], down_weight[0])
    summed = lax.psum(partial_value, "local")
    mine = lax.dynamic_slice_in_dim(summed, lax.axis_index("local") * width, width, 1)
    d_rows = mine.astype(jnp.bfloat16)
    return lax.psum_scatter(
        lax.dot_general(
            sel_half, d_rows, (((0,), (0,)), ((), ())), preferred_element_type=jnp.float32
        ),
        "node",
        scatter_dimension=0,
        tiled=True,
    ).astype(jnp.bfloat16)


def solution(mesh):
    placed = (
        P("node", "local"),
        P("node", "local"),
        P(),
        P(),
        P("node", None, "local"),
        P("node", None, "local"),
        P("node", "local", None),
    )
    return jax.shard_map(
        shards, mesh=mesh, in_specs=placed, out_specs=P("node", "local"), check_vma=False
    )
```

profile of v0, /device:TPU:0, one launch (start us, length us, event | category | flops | bytes accessed | tf_op | source)
XLA Modules:
  0.0 141.6 jit_solution(6451418618623909036)
XLA Ops:
  0.0 0.8 broadcast_compare_fusion
  0.8 0.1 copy.17
  0.9 0.1 reshape.51
  1.1 0.3 reduce-window_clone.1
  1.4 0.1 sub.10
  1.5 0.1 copy.18
  1.6 1.0 select_reduce_fusion
  2.6 32.6 %all_gather.12 = bf16[64,896]{1,0:T(8,128)(2,1)S(1)} all-gather(bf16[8,896]{1,0:T(8,128)(2,1)} %param.8), channel_id=1, replica_groups=mesh['node'=8,'local'=4] {'node'}, dimensions={0}, use_global_device_ids=true | all-gather | bytes 129024 | tf_op jit(solution)/shard_map/all_gather | solution.py:49
  35.2 0.1 fusion.9
  35.3 5.7 %all_gather.13 = bf16[32,3584]{1,0:T(8,128)(2,1)S(1)} all-gather(bf16[32,896]{1,0:T(8,128)(2,1)S(1)} %fusion.9), channel_id=1, replica_groups=mesh['node'=8,'local'=4] {'local'}, dimensions={1}, use_global_device_ids=true | all-gather | bytes 286720 | tf_op jit(solution)/shard_map/all_gather | solution.py:57
  41.0 2.1 %fusion.7 = f32[32,256]{1,0:T(8,128)S(1)} fusion(bf16[32,3584]{1,0:T(8,128)(2,1)S(1)} %all_gather.13, bf16[1,256,3584]{2,1,0:T(8,128)(2,1)} %param.13), kind=kOutput, calls=%fused_computation.8 | convolution fusion | flops 58720256 | bytes 2097152 | tf_op jit(solution)/shard_map/dot_general | solution.py:26
  43.1 0.0 copy-done.2
  43.2 30.6 %all_gather.14 = bf16[64,896]{1,0:T(8,128)(2,1)S(1)} all-gather(bf16[8,896]{1,0:T(8,128)(2,1)S(1)} %copy-done.2), channel_id=1, replica_groups=mesh['node'=8,'local'=4] {'node'}, dimensions={0}, use_global_device_ids=true | all-gather | bytes 129024 | tf_op jit(solution)/shard_map/all_gather | solution.py:48
  73.7 0.1 convolution_convert_fusion
  73.9 5.7 %all_gather.15 = bf16[32,3584]{1,0:T(8,128)(2,1)S(1)} all-gather(bf16[32,896]{1,0:T(8,128)(2,1)S(1)} %convolution_convert_fusion), channel_id=1, replica_groups=mesh['node'=8,'local'=4] {'local'}, dimensions={1}, use_global_device_ids=true | all-gather | bytes 286720 | tf_op jit(solution)/shard_map/all_gather | solution.py:56
  79.6 0.4 fusion.2
  80.0 0.0 copy-done
  80.0 2.8 %fusion = f32[32,3584]{1,0:T(8,128)S(1)} fusion(bf16[1,3584,256]{2,1,0:T(8,128)(2,1)} %param.11, f32[32,256]{1,0:T(8,128)S(1)} %fusion.7, bf16[32,3584]{1,0:T(8,128)(2,1)S(1)} %all_gather.15, bf16[1,3584,256]{2,1,0:T(8,128)(2,1)S(1)} %copy-done, f32[32,256]{1,0:T(8,128)S(1)} %fusion.2), kind=kOutput, calls=%fused_computation.1 | convolution fusion | flops 117522432 | bytes 4423680 | tf_op jit(solution)/shard_map/dot_general | solution.py:31
  82.8 0.7 convolution_add_fusion
  83.5 16.3 %all-reduce.3 = bf16[32,3584]{1,0:T(8,128)(2,1)S(1)} all-reduce(f32[32,3584]{1,0:T(8,128)S(1)} %convolution_add_fusion), channel_id=1, replica_groups=mesh['node'=8,'local'=4] {'local'}, use_global_device_ids=true, to_apply=%region_3.4 | all-reduce | flops 114688 | bytes 688128 | tf_op jit(solution)/shard_map/psum | solution.py:60
  99.8 0.2 fusion.24
  100.0 39.7 %all-reduce.4 = bf16[64,896]{1,0:T(8,128)(2,1)S(1)} all-reduce(f32[64,896]{1,0:T(8,128)S(1)} %fusion.24), channel_id=2, replica_groups=mesh['node'=8,'local'=4] {'node'}, use_global_device_ids=true, to_apply=%region_4.5.clone | all-reduce | flops 57344 | bytes 344064
  139.8 0.6 dynamic-slice
  141.0 0.6 dynamic-slice_convert_fusion.2
  (7 shorter events, 0.0 us)
Async XLA Ops:
  0.0 80.0 %copy-start = (bf16[1,3584,256]{2,1,0:T(8,128)(2,1)S(1)}, bf16[1,3584,256]{2,1,0:T(8,128)(2,1)}, u32[]{:S(2)}) copy-start(bf16[1,3584,256]{2,1,0:T(8,128)(2,1)} %param.12) | copy-start | bytes 5505028
  0.0 43.1 %copy-start.2 = (bf16[8,896]{1,0:T(8,128)(2,1)S(1)}, bf16[8,896]{1,0:T(8,128)(2,1)}, u32[]{:S(2)}) copy-start(bf16[8,896]{1,0:T(8,128)(2,1)} %param.7) | copy-start | bytes 43012
  1.6 78.0 %copy-start.1 = (bf16[1,3584,256]{2,1,0:T(8,128)(2,1)S(1)}, bf16[1,3584,256]{2,1,0:T(8,128)(2,1)}, u32[]{:S(2)}) copy-start(bf16[1,3584,256]{2,1,0:T(8,128)(2,1)} %param.11) | copy-start | bytes 5505028
  82.8 56.9 %copy-start.3 = (u32[32]{0:T(128)S(1)}, u32[32]{0:T(128)}, u32[]{:S(2)}) copy-start(u32[32]{0:T(128)} %constant.33) | copy-start | bytes 388
where the time goes:
time: 142 us
  blocking collectives  131 us (92%)
  matrix products  6.46 us (5%)
  other arithmetic  2.11 us (1%)
  local copies, waits for them, and re-layouts  1.68 us (1%)
    unnamed x1, blocking collectives  39.7 us
    all_gather x1, blocking collectives, shards(): lax.all_gather(out_grad, 'node', axis=0, tiled=True)  32.6 us
    all_gather x1, blocking collectives, shards(): lax.all_gather(inputs, 'node', axis=0, tiled=True)  30.6 us
    psum x1, blocking collectives, shards(): summed = lax.psum(partial_value, 'local')  16.3 us
    all_gather x1, blocking collectives, shards(): lax.all_gather(g_part, 'local', axis=1, tiled=True)  5.69 us
    all_gather x1, blocking collectives, shards(): lax.all_gather(x_part, 'local', axis=1, tiled=True)  5.69 us

commit v1 on v0

--- a/solution.py
+++ b/solution.py
@@ -57,7 +57,7 @@
         lax.all_gather(g_part, "local", axis=1, tiled=True),
     )
     partial_value = expert_terms(x_rows, g_rows, gate_weight[0], up_weight[0], down_weight[0])
-    summed = lax.psum(partial_value, "local")
+    summed = lax.all_gather(partial_value, axis_name="local").sum(axis=0)
     mine = lax.dynamic_slice_in_dim(summed, lax.axis_index("local") * width, width, 1)
     d_rows = mine.astype(jnp.bfloat16)
     return lax.psum_scatter(

time: 142 us -> 163 us (1.15)
  waiting for transfers between devices: 0 us -> 20.9 us
  blocking collectives: 131 us -> 115 us
  between operations: 0.74 us -> 14.1 us
    all_gather x0 -> x1, waiting for transfers between devices: none -> 20.9 us  [shards(): summed = lax.all_gather(partial_value, axis_name='local').sum(axis=0)]
    psum x1 -> x0, blocking collectives: 16.3 us -> none  [shards(): summed = lax.psum(partial_value, 'local')]
    reduce_sum x0 -> x1, other arithmetic: none -> 1.63 us  [shards(): summed = lax.all_gather(partial_value, axis_name='local').sum(axis=0)]
  transfers between devices with their start and end apart: 0 -> 1, of which waited for: 0 -> 1; matrix products, arithmetic and copies ran while one was open for 0% -> 0% of each run, Pallas kernels for 0% -> 0%
where the time goes in v1:
time: 163 us; the launch traced here: 162 us
  blocking collectives  115 us (71%)
  waiting for transfers between devices  20.9 us (13%)
  between operations  14.1 us (9%)
  matrix products  7.26 us (4%)
  other arithmetic  3.58 us (2%)
  local copies, waits for them, and re-layouts  1.68 us (1%)
    unnamed x1, blocking collectives  39.9 us
    all_gather x1, blocking collectives, shards(): lax.all_gather(out_grad, 'node', axis=0, tiled=True)  32.8 us
    all_gather x1, blocking collectives, shards(): lax.all_gather(inputs, 'node', axis=0, tiled=True)  30.8 us
    all_gather x1, waiting for transfers between devices, shards(): summed = lax.all_gather(partial_value, axis_name='local').sum(axis=0)  20.9 us
    all_gather x1, blocking collectives, shards(): lax.all_gather(g_part, 'local', axis=1, tiled=True)  5.69 us
    all_gather x1, blocking collectives, shards(): lax.all_gather(x_part, 'local', axis=1, tiled=True)  5.69 us
  transfers between devices with their start and end apart: 1, of which 1 were waited for; matrix products, arithmetic and copies ran while one was open for 0% of the time, Pallas kernels for 0%

profile of v1, /device:TPU:0, one launch (start us, length us, event | category | flops | bytes accessed | tf_op | source)
XLA Modules:
  0.0 162.3 jit_solution(952884830850161775)
XLA Ops:
  6.5 0.8 broadcast_compare_fusion
  7.4 0.1 copy.17
  7.5 0.1 reshape.51
  7.6 0.3 reduce-window_clone.1
  7.9 0.1 sub.10
  8.1 0.1 copy.18
  8.1 32.8 %all_gather.18 = bf16[64,896]{1,0:T(8,128)(2,1)S(1)} all-gather(bf16[8,896]{1,0:T(8,128)(2,1)} %param.8), channel_id=1, replica_groups=mesh['node'=8,'local'=4] {'node'}, dimensions={0}, use_global_device_ids=true | all-gather | bytes 129024 | tf_op jit(solution)/shard_map/all_gather | solution.py:49
  40.9 0.8 select_reduce_fusion
  41.7 0.1 fusion.9
  41.8 5.7 %all_gather.19 = bf16[32,3584]{1,0:T(8,128)(2,1)S(1)} all-gather(bf16[32,896]{1,0:T(8,128)(2,1)S(1)} %fusion.9), channel_id=1, replica_groups=mesh['node'=8,'local'=4] {'local'}, dimensions={1}, use_global_device_ids=true | all-gather | bytes 286720 | tf_op jit(solution)/shard_map/all_gather | solution.py:57
  47.5 30.8 %all_gather.20 = bf16[64,896]{1,0:T(8,128)(2,1)S(1)} all-gather(bf16[8,896]{1,0:T(8,128)(2,1)} %param.7), channel_id=1, replica_groups=mesh['node'=8,'local'=4] {'node'}, dimensions={0}, use_global_device_ids=true | all-gather | bytes 129024 | tf_op jit(solution)/shard_map/all_gather | solution.py:48
  78.3 0.1 convolution_convert_fusion
  78.5 5.7 %all_gather.21 = bf16[32,3584]{1,0:T(8,128)(2,1)S(1)} all-gather(bf16[32,896]{1,0:T(8,128)(2,1)S(1)} %convolution_convert_fusion), channel_id=1, replica_groups=mesh['node'=8,'local'=4] {'local'}, dimensions={1}, use_global_device_ids=true | all-gather | bytes 286720 | tf_op jit(solution)/shard_map/all_gather | solution.py:56
  84.2 2.1 %fusion.7 = f32[32,256]{1,0:T(8,128)S(1)} fusion(bf16[32,3584]{1,0:T(8,128)(2,1)S(1)} %all_gather.19, bf16[1,256,3584]{2,1,0:T(8,128)(2,1)} %param.13), kind=kOutput, calls=%fused_computation.8 | convolution fusion | flops 58720256 | bytes 2097152 | tf_op jit(solution)/shard_map/dot_general | solution.py:26
  86.3 0.0 copy-done.1
  86.3 0.4 fusion.2
  86.7 2.8 %fusion = f32[32,3584]{1,0:T(8,128)S(1)} fusion(bf16[1,3584,256]{2,1,0:T(8,128)(2,1)} %param.11, f32[32,256]{1,0:T(8,128)S(1)} %fusion.7, bf16[32,3584]{1,0:T(8,128)(2,1)S(1)} %all_gather.21, bf16[1,3584,256]{2,1,0:T(8,128)(2,1)S(1)} %copy-done, f32[32,256]{1,0:T(8,128)S(1)} %fusion.2), kind=kOutput, calls=%fused_computation.1 | convolution fusion | flops 117522432 | bytes 4423680 | tf_op jit(solution)/shard_map/dot_general | solution.py:31
  89.6 1.4 convolution_add_fusion
  91.0 0.6 dynamic-slice
  92.3 20.9 %all-gather.3.cloned.1.call-done = f32[128,3584]{1,0:T(8,128)} async-done(((f32[32,3584]{1,0:T(8,128)}), f32[128,3584]{1,0:T(8,128)}) %all-gather.3.cloned.1.call-update) | async-done | bytes 1835024 | tf_op jit(solution)/shard_map/all_gather | solution.py:60
  113.1 1.6 %reduce_sum.29 = bf16[32,3584]{1,0:T(8,128)(2,1)S(1)} reduce(f32[4,32,3584]{2,1,0:T(8,128)} %bitcast.33, f32[]{:T(128)} %constant.24.clone.1), dimensions={0}, to_apply=%region_3.4 | reduce | flops 344064 | bytes 2064388 | tf_op jit(solution)/shard_map/reduce_sum | solution.py:60
  114.8 0.2 fusion.24
  115.0 39.9 %all-reduce.2 = bf16[64,896]{1,0:T(8,128)(2,1)S(1)} all-reduce(f32[64,896]{1,0:T(8,128)S(1)} %fusion.24), channel_id=3, replica_groups=mesh['node'=8,'local'=4] {'node'}, use_global_device_ids=true, to_apply=%region_4.5.clone | all-reduce | flops 57344 | bytes 344064
  154.9 0.6 dynamic-slice_convert_fusion.2
  (8 shorter events, 0.1 us)
Async XLA Ops:
  6.5 80.2 %copy-start = (bf16[1,3584,256]{2,1,0:T(8,128)(2,1)S(1)}, bf16[1,3584,256]{2,1,0:T(8,128)(2,1)}, u32[]{:S(2)}) copy-start(bf16[1,3584,256]{2,1,0:T(8,128)(2,1)} %param.12) | copy-start | bytes 5505028
  6.5 106.6 %all-gather.3.cloned.1.call-start = ((), (), s32[]{:S(2)}) async-start(), calls=%async_computation | async-start | bytes 2293760 | tf_op jit(solution)/shard_map/all_gather | solution.py:60
  8.1 78.1 %copy-start.1 = (bf16[1,3584,256]{2,1,0:T(8,128)(2,1)S(1)}, bf16[1,3584,256]{2,1,0:T(8,128)(2,1)}, u32[]{:S(2)}) copy-start(bf16[1,3584,256]{2,1,0:T(8,128)(2,1)} %param.11) | copy-start | bytes 5505028
  89.6 1.5 copy-start.2
Sparse Core Ops, SparseCore 0:
  91.1 21.9 all-gather.2
